TPU v7x, 256 devices: a whole 4x4x8 slice. The times are simulated.
256 devices in a mesh: dp: 64 (over z, x, y_hi), tensor: 4 (over y_lo, core).
Axes of the slice: x: 4, y: 4 (y_hi: 2, y_lo: 2; y = y_hi * 2 + y_lo), z: 8, core: 2. Of those that a mesh axis runs over, the one named last changes fastest.
Arguments:
- d_out: bfloat16 [16384, 3072], P('dp'), may hold values from -12 to 12
- gate: bfloat16 [16384, 4096], P('dp', 'tensor'), may hold values from -16 to 16
- up_proj: bfloat16 [16384, 4096], P('dp', 'tensor'), may hold values from -12 to 12
- master: float32 [4096, 3072], P(('tensor', 'dp')), may hold values from -0.09375 to 0.09375
- moment_one: float32 [4096, 3072], P(('tensor', 'dp')), may hold values from -4 to 4
- moment_two: float32 [4096, 3072], P(('tensor', 'dp')), may hold values from 0.05 to 2
Outputs:
- gate_grad: bfloat16 [16384, 4096], P('dp', 'tensor')
- up_grad: bfloat16 [16384, 4096], P('dp', 'tensor')
- master_next: float32 [4096, 3072], P(('tensor', 'dp'))
- moment_one_next: float32 [4096, 3072], P(('tensor', 'dp'))
- moment_two_next: float32 [4096, 3072], P(('tensor', 'dp'))
- weight_next: bfloat16 [4096, 3072], P('tensor')
All inputs are finite; a program needn't handle non-finite values.
Results may differ from a plain program's by a relative error of at most 0.005.
Values may be sent and summed in bfloat16 or wider, within the bound.
A program may use at most 64 MiB of HBM per device.

v0:
```python
import jax
import jax.numpy as jnp
from jax import lax
from jax.sharding import PartitionSpec as P

D = 3072
FF = 4096


def on_device(d_out, gate, up_proj, master, moment_one, moment_two):
    weight = master.astype(jnp.bfloat16)
    gate_f = gate.astype(jnp.float32)
    up_f = up_proj.astype(jnp.float32)
    silu_gate = jax.nn.silu(gate_f)
    hidden = (silu_gate * up_f).astype(jnp.bfloat16)
    d_hidden = lax.dot_general(
        d_out,
        lax.all_gather(weight, "dp", axis=0, tiled=True),
        (((1,), (1,)), ((), ())),
        preferred_element_type=jnp.float32,
    )
    partial_term = lax.dot_general(
        hidden, d_out, (((0,), (0,)), ((), ())), preferred_element_type=jnp.float32
    )
    grad = lax.psum_scatter(partial_term, "dp", scatter_dimension=0, tiled=True)
    up_grad = (d_hidden * silu_gate).astype(jnp.bfloat16)
    sigm = jax.nn.sigmoid(gate_f)
    gate_grad = (d_hidden * up_f * sigm * (1.0 + gate_f * (1.0 - sigm))).astype(jnp.bfloat16)
    local_squares = jnp.sum(grad * grad)
    total = lax.psum(local_squares, ("dp", "tensor"))
    factor = 1.0 / jnp.sqrt(total / (FF * D) + 1e-06)
    clipped = grad * factor
    moment_one_next = 0.9 * moment_one + 0.1 * clipped
    moment_two_next = 0.95 * moment_two + 0.05 * clipped * clipped
    master_next = master - 0.003 * (
        moment_one_next / (jnp.sqrt(moment_two_next) + 1e-08) + 0.1 * master
    )
    shard_next = master_next.astype(jnp.bfloat16)
    weight_next = lax.all_gather(shard_next, "dp", axis=0, tiled=True)
    return (gate_grad, up_grad, master_next, moment_one_next, moment_two_next, weight_next)


def solution(mesh):
    placed = (
        P("dp", None),
        P("dp", "tensor"),
        P("dp", "tensor"),
        P(("tensor", "dp"), None),
        P(("tensor", "dp"), None),
        P(("tensor", "dp"), None),
    )
    return jax.shard_map(
        on_device,
        mesh=mesh,
        in_specs=placed,
        out_specs=(
            P("dp", "tensor"),
            P("dp", "tensor"),
            P(("tensor", "dp"), None),
            P(("tensor", "dp"), None),
            P(("tensor", "dp"), None),
            P("tensor", None),
        ),
        check_vma=False,
    )
```

profile of v0, /device:TPU:8, one launch (start us, length us, event | category | flops | bytes accessed | tf_op | source)
XLA Modules:
  0.0 1211.7 jit_solution(3031577703967708781)
XLA Ops:
  7.2 0.0 copy-start
  7.2 0.0 reduce-scatter.2.cloned.1.call-start
  7.2 1.4 copy-done
  8.6 7.7 fusion.8
  16.3 0.0 copy-start.3
  16.3 0.0 copy-start.2
  16.3 0.0 reduce-scatter.2.cloned.1.call-update
  16.3 0.0 all-gather.3.cloned.1.call-start
  16.4 832.4 %reduce-scatter.2.cloned.1.call-done = f32[16,3072]{1,0:T(8,128)} async-done(((f32[1024,3072]{1,0:T(8,128)}), f32[16,3072]{1,0:T(8,128)}) %reduce-scatter.2.cloned.1.call-update) | async-done | bytes 196624 | tf_op jit(solution)/shard_map/reduce_scatter | solution.py:25
  848.7 1.6 multiply_reduce_fusion
  850.3 73.3 %psum.7 = f32[]{:T(128)} all-reduce(f32[]{:T(128)} %multiply_reduce_fusion), channel_id=1, replica_groups=mesh['dp'=64,'tensor'=4] {'dp','tensor'}, use_global_device_ids=true, to_apply=%region_2.3 | all-reduce | flops 1 | bytes 8 | tf_op jit(solution)/shard_map/psum | solution.py:30
  924.3 0.0 copy-done.3
  924.3 0.0 copy-done.4
  924.3 0.0 copy-done.5
  924.3 1.9 fusion.12
  926.2 0.0 all-gather.3.cloned.1.call-update
  926.2 0.0 all-gather.5.cloned.1.call-start
  926.3 0.7 all-gather.5.cloned.1.call-update
  927.0 133.8 %all-gather.3.cloned.1.call-done = bf16[1024,3072]{1,0:T(8,128)(2,1)} async-done(((bf16[16,3072]{1,0:T(8,128)(2,1)}), bf16[1024,3072]{1,0:T(8,128)(2,1)}) %all-gather.3.cloned.1.call-update) | async-done | bytes 6291472 | tf_op jit(solution)/shard_map/all_gather | solution.py:18
  1060.8 0.0 copy-done.1
  1060.8 0.0 copy-done.2
  1060.8 5.9 multiply_convert_fusion
  1066.7 132.6 %all-gather.5.cloned.1.call-done = bf16[1024,3072]{1,0:T(8,128)(2,1)} async-done(((bf16[16,3072]{1,0:T(8,128)(2,1)}), bf16[1024,3072]{1,0:T(8,128)(2,1)}) %all-gather.5.cloned.1.call-update) | async-done | bytes 6291472 | tf_op jit(solution)/shard_map/all_gather | solution.py:39
  1199.3 5.9 copy.13
  (3 shorter events, 0.0 us)
Async XLA Ops:
  7.2 1.4 copy-start
  7.2 841.5 %reduce-scatter.2.cloned.1.call-start = ((), (), s32[]{:S(2)}) async-start(), calls=%async_computation.2 | async-start | bytes 12779520 | tf_op jit(solution)/shard_map/reduce_scatter | solution.py:25
  16.3 908.1 %copy-start.3 = (f32[16,3072]{1,0:T(8,128)S(1)}, f32[16,3072]{1,0:T(8,128)}, u32[]{:S(2)}) copy-start(f32[16,3072]{1,0:T(8,128)} %param.9) | copy-start | bytes 589828
  16.3 908.1 %copy-start.4 = (f32[16,3072]{1,0:T(8,128)S(1)}, f32[16,3072]{1,0:T(8,128)}, u32[]{:S(2)}) copy-start(f32[16,3072]{1,0:T(8,128)} %param.11) | copy-start | bytes 589828
  16.3 908.1 %copy-start.5 = (f32[16,3072]{1,0:T(8,128)S(1)}, f32[16,3072]{1,0:T(8,128)}, u32[]{:S(2)}) copy-start(f32[16,3072]{1,0:T(8,128)} %param.10) | copy-start | bytes 589828
  16.3 1044.5 %copy-start.1 = (bf16[256,1024]{1,0:T(8,128)(2,1)S(1)}, bf16[256,1024]{1,0:T(8,128)(2,1)}, u32[]{:S(2)}) copy-start(bf16[256,1024]{1,0:T(8,128)(2,1)} %param.7) | copy-start | bytes 1572868
  16.3 1044.5 %copy-start.2 = (bf16[256,1024]{1,0:T(8,128)(2,1)S(1)}, bf16[256,1024]{1,0:T(8,128)(2,1)}, u32[]{:S(2)}) copy-start(bf16[256,1024]{1,0:T(8,128)(2,1)} %param.8) | copy-start | bytes 1572868
  16.3 1044.5 %all-gather.3.cloned.1.call-start = ((), (), s32[]{:S(2)}) async-start(), calls=%async_computation.1 | async-start | bytes 6389760 | tf_op jit(solution)/shard_map/all_gather | solution.py:18
  926.2 273.0 %all-gather.5.cloned.1.call-start = ((), (), s32[]{:S(2)}) async-start(), calls=%async_computation.3 | async-start | bytes 6389760 | tf_op jit(solution)/shard_map/all_gather | solution.py:39
Sparse Core Ops, SparseCore 0:
  16.4 832.2 reduce-scatter.1
  926.4 134.3 all-gather.2
  1065.6 133.6 all-gather.4
where the time goes:
time: 1210 us
  waiting for transfers between devices  1100 us (91%)
  blocking collectives  73.3 us (6%)
  between operations  14.5 us (1%)
  matrix products  13.6 us (1%)
    reduce_scatter x1, waiting for transfers between devices, on_device(): grad = lax.psum_scatter(partial_term, 'dp', scatter_dimension=0, tiled=True)  832 us
    all_gather x1, waiting for transfers between devices, on_device(): lax.all_gather(weight, 'dp', axis=0, tiled=True)  134 us
    all_gather x1, waiting for transfers between devices, on_device(): weight_next = lax.all_gather(shard_next, 'dp', axis=0, tiled=True)  133 us
    psum x1, blocking collectives, on_device(): total = lax.psum(local_squares, ('dp', 'tensor'))  73.3 us
  transfers between devices with their start and end apart: 3, of which 3 were waited for; matrix products, arithmetic and copies ran while one was open for 0% of the time, Pallas kernels for 0%

commit v1 on v0

v1 whole, which is shorter than its diff:
```python
import functools

import jax
import jax.numpy as jnp
from jax import lax
from jax.experimental import pallas as pl
from jax.experimental.pallas import tpu as pltpu
from jax.sharding import PartitionSpec as P

D = 3072
FF = 4096
MESH = pl.DeviceIdType.MESH
F32 = jnp.float32
BF16 = jnp.bfloat16

RS_A = ((0, 640), (1536, 640))
RS_B = ((640, 896), (2176, 896))
CHUNKS = (RS_A[0], RS_B[0], RS_A[1], RS_B[1])
AG_A = ((0, 768), (768, 768))
AG_B = (1536, 1536)

N_GATHER = 2 * (3 + 8) + 8 + 24
N_COPIES = 2 * N_GATHER + 10 + 2 * (8 + 3) + 2 * (3 + 7) + 17 + 1


def kernel(
    d_in, g_in, u_in, ma_in, m1_in, m2_in,
    gg_o, ug_o, ma_o, m1_o, m2_o, w_o,
    d2, gv, uv, mav, m1v, m2v, wg, ht, hr, gr,
    sah, rah, sa, ra, sax, rax, acca, sb, rb, accb, sbz, rbz,
    g, sq, rz, rx, ry, dh, dhs, ob, ggv, ugv,
    ssem, rsem, lsem,
):
    dp, tensor = lax.axis_index("dp"), lax.axis_index("tensor")
    z, x, h = dp // 8, (dp // 2) % 4, dp % 2
    yl, c = tensor // 2, tensor % 2
    y = 2 * h + yl

    def device(zz, xx, yy, cc):
        return (zz * 8 + xx * 2 + yy // 2, (yy % 2) * 2 + cc)

    def at_z(k):
        return device((z + k + 8) % 8, x, y, c)

    def at_x(k):
        return device(z, (x + k + 4) % 4, y, c)

    across = device(z, x, 3 - y, c)
    mate = device(z, x, y, 1 - c)
    pair = (z * 8 + x * 2 + 1 - h, tensor)

    def near(k):
        i = (y * 2 + c + k) % 8
        return device(z, x, i // 2, i % 2)

    count = [0]
    sent = []

    def send(src, dst, to):
        i = count[0]
        count[0] += 1
        copy = pltpu.make_async_remote_copy(
            src_ref=src, dst_ref=dst, send_sem=ssem.at[i], recv_sem=rsem.at[i],
            device_id=to, device_id_type=MESH,
        )
        copy.start()
        sent.append(copy)
        return copy

    def load(src, dst, i):
        copy = pltpu.make_async_copy(src, dst, lsem.at[i])
        copy.start()
        return copy

    load_ma = load(ma_in, mav, 0)
    load_g = load(g_in, gv, 1)
    load_u = load(u_in, uv, 2)
    load_d = load(d_in, d2.at[0], 3)
    load_m1 = load(m1_in, m1v, 4)
    load_m2 = load(m2_in, m2v, 5)

    barrier = pltpu.get_barrier_semaphore()
    friends = (
        [at_z(k) for k in range(1, 8)]
        + [at_x(k) for k in range(1, 4)]
        + [near(k) for k in range(1, 8)]
    )
    for friend in friends:
        pl.semaphore_signal(barrier, inc=1, device_id=friend, device_id_type=MESH)
    load_ma.wait()
    wg[z, x] = mav[...].astype(BF16)
    load_d.wait()
    pl.semaphore_wait(barrier, len(friends))

    class Gather:
        def __init__(self, buf):
            self.buf = buf

        def start(self):
            buf = self.buf
            self.ax = []
            for c0, w in AG_A:
                own = buf.at[z, x, :, pl.ds(c0, w)]
                self.ax.append([send(own, own, at_x(k)) for k in (1, 3, 2)])
            self.bz = [None] * 4
            self.bx = []
            self.az = [[None] * 4 for _ in AG_A]
            self.b_step(1)
            self.b_spread(z)

        def b_spread(self, zz):
            c0, w = AG_B
            block = self.buf.at[zz, x, :, pl.ds(c0, w)]
            self.bx += [send(block, block, at_x(k)) for k in (1, 3, 2)]

        def b_step(self, s):
            c0, w = AG_B
            pieces = ((c0, w), (c0, w)) if s < 4 else ((c0, w // 2), (c0 + w // 2, w // 2))
            up = self.buf.at[(z - s + 9) % 8, x, :, pl.ds(*pieces[0])]
            down = self.buf.at[(z + s - 1) % 8, x, :, pl.ds(*pieces[1])]
            self.bz[s - 1] = [send(up, up, at_z(1)), send(down, down, at_z(-1))]

        def b_next(self, s):
            for copy in self.bz[s - 1]:
                copy.wait_recv()
            if s < 4:
                self.b_step(s + 1)
                self.b_spread((z - s + 8) % 8)
                self.b_spread((z + s) % 8)
            else:
                self.b_spread((z + 4) % 8)

        def a_step(self, j, s):
            cols = pl.ds(*AG_A[j])
            a, b = (pl.ds(0, 4), pl.ds(0, 4)) if s < 4 else (pl.ds(0, 2), pl.ds(2, 2))
            up = self.buf.at[(z - s + 9) % 8, a, :, cols]
            down = self.buf.at[(z + s - 1) % 8, b, :, cols]
            self.az[j][s - 1] = [send(up, up, at_z(1)), send(down, down, at_z(-1))]

        def a_next(self, j, s):
            for copy in self.ax[j] if s == 0 else self.az[j][s - 1]:
                copy.wait_recv()
            if s < 4:
                self.a_step(j, s + 1)

        def finish(self):
            for copy in self.bx:
                copy.wait_recv()

    wga = Gather(wg)
    wga.start()

    half = pl.ds(pl.multiple_of(c * 128, 128), 128)
    cross = [
        send(d2.at[0, half, pl.ds(c0, w)], d2.at[1, half, pl.ds(c0, w)], across)
        for c0, w in CHUNKS
    ]
    swap = [None] * 4

    def pass_on(k):
        cross[k].wait_recv()
        block = d2.at[1, half, pl.ds(*CHUNKS[k])]
        swap[k] = send(block, block, mate)

    load_g.wait()
    load_u.wait()
    for i in range(8):
        cols = pl.ds(i * 128, 128)
        gate = gv[:, cols].astype(F32)
        hidden = gate * jax.nn.sigmoid(gate) * uv[:, cols].astype(F32)
        turned = hidden.astype(BF16).astype(F32).T.astype(BF16)
        for j in range(8):
            ht[j % 2, pl.ds((4 * i + j // 2) * 16, 16), :] = turned[j * 16 : j * 16 + 16, :]
    hid = send(ht.at[1 - h], hr, pair)

    wga.a_next(0, 0)
    wga.a_next(1, 0)
    wga.b_next(1)
    pass_on(0)
    wga.b_next(2)
    pass_on(1)
    wga.a_next(0, 1)
    hid.wait_recv()

    def partial_sums(k):
        c0, w = CHUNKS[k]
        swap[k].wait_recv()
        for i in range(4):
            rows = pl.ds(i * 128, 128)
            acc = jnp.dot(ht[h, rows, :], d2[0, :, pl.ds(c0, w)], preferred_element_type=F32)
            acc += jnp.dot(hr[rows, :], d2[1, :, pl.ds(c0, w)], preferred_element_type=F32)
            gr[pl.ds(2 * i, 2), :, :, pl.ds(c0, w)] = acc.reshape(2, 4, 16, w)

    ring = [[[None, None] for _ in range(4)] for _ in RS_A]
    last_x = [None] * 2

    def a_send(j, s):
        cols = pl.ds(*RS_A[j])
        for way, sign in ((0, 1), (1, -1)):
            to = (z + sign * (5 - s) + 8) % 8
            if s == 1:
                part = pl.ds(2 * way, 2)
                sah[j, way] = gr[to, part, :, cols].astype(BF16)
                ring[j][0][way] = send(sah.at[j, way], rah.at[j, way], at_z(sign))
                continue
            ring[j][s - 2][way].wait_recv()
            if s == 2:
                part, rest = pl.ds(2 * way, 2), pl.ds(2 - 2 * way, 2)
                sa[j, way, 0, part] = (gr[to, part, :, cols] + rah[j, way].astype(F32)).astype(BF16)
                sa[j, way, 0, rest] = gr[to, rest, :, cols].astype(BF16)
            else:
                sa[j, way, s - 2] = (gr[to, :, :, cols] + ra[j, way, s - 3].astype(F32)).astype(BF16)
            ring[j][s - 1][way] = send(sa.at[j, way, s - 2], ra.at[j, way, s - 2], at_z(sign))

    def a_turn(j):
        cols = pl.ds(*RS_A[j])
        for way in (0, 1):
            ring[j][3][way].wait_recv()
        acca[j] = gr[z, :, :, cols] + ra[j, 0, 2].astype(F32) + ra[j, 1, 2].astype(F32)
        last_x[j] = []
        for k in (1, 3, 2):
            sax[j, k - 1] = acca[j, (x + k) % 4].astype(BF16)
            last_x[j].append(send(sax.at[j, k - 1], rax.at[j, k - 1], at_x(k)))

    def a_end(j):
        for copy in last_x[j]:
            copy.wait_recv()
        total = acca[j, x]
        for k in range(3):
            total += rax[j, k].astype(F32)
        g[:, pl.ds(*RS_A[j])] = total

    first_x = [None] * 2
    last_z = [None] * 2

    def b_send(j):
        first_x[j] = []
        for k in (1, 3, 2):
            sb[j, k - 1] = gr[:, (x + k) % 4, :, pl.ds(*RS_B[j])].astype(BF16)
            first_x[j].append(send(sb.at[j, k - 1], rb.at[j, k - 1], at_x(k)))

    def b_turn(j):
        for copy in first_x[j]:
            copy.wait_recv()
        total = gr[:, x, :, pl.ds(*RS_B[j])]
        for k in range(3):
            total += rb[j, k].astype(F32)
        accb[j] = total
        last_z[j] = []
        for k in (4, 3, 5, 2, 6, 1, 7):
            sbz[j, k - 1] = accb[j, (z + k) % 8].astype(BF16)
            last_z[j].append(send(sbz.at[j, k - 1], rbz.at[j, k - 1], at_z(k)))

    def b_end(j):
        for copy in last_z[j]:
            copy.wait_recv()
        total = accb[j, z]
        for k in range(7):
            total += rbz[j, k].astype(F32)
        g[:, pl.ds(*RS_B[j])] = total

    partial_sums(0)
    a_send(0, 1)
    wga.a_next(1, 1)
    wga.b_next(3)
    pass_on(2)
    partial_sums(1)
    b_send(0)
    wga.b_next(4)
    a_send(0, 2)
    wga.a_next(0, 2)
    pass_on(3)
    partial_sums(2)
    a_send(1, 1)
    wga.a_next(1, 2)
    a_send(0, 3)
    partial_sums(3)
    b_send(1)
    a_send(1, 2)
    wga.a_next(0, 3)
    wga.a_next(1, 3)
    a_send(0, 4)
    a_send(1, 3)
    b_turn(0)
    a_turn(0)
    a_send(1, 4)
    b_turn(1)
    a_turn(1)
    b_end(0)
    a_end(0)
    b_end(1)
    a_end(1)

    square = g[...] * g[...]
    square = square[:8] + square[8:]
    total = square[:, 0:128]
    for i in range(1, 24):
        total += square[:, i * 128 : i * 128 + 128]
    sq[0] = total
    load_m1.wait()
    load_m2.wait()
    hops = [send(sq.at[0], rz.at[k - 1], at_z(k)) for k in (4, 3, 5, 2, 6, 1, 7)]

    def d_hidden(j):
        for i in range(4):
            part = lax.dot_general(
                wg[pl.ds(2 * i, 2)].reshape(128, D), d2[j],
                (((1,), (1,)), ((), ())), preferred_element_type=F32,
            )
            if j == 0:
                dh[h, pl.ds(i * 128, 128), :] = part
            else:
                dhs[pl.ds(i * 128, 128), :] = part

    wga.a_next(0, 4)
    wga.a_next(1, 4)
    wga.finish()
    for copy in hops:
        copy.wait_recv()
    for k in range(7):
        total += rz[k]
    sq[1] = total
    hops = [send(sq.at[1], rx.at[k - 1], at_x(k)) for k in (2, 1, 3)]
    d_hidden(1)
    for copy in hops:
        copy.wait_recv()
    for k in range(3):
        total += rx[k]
    sq[2] = total
    hops = [send(sq.at[2], ry.at[k - 1], near(k)) for k in (4, 3, 5, 2, 6, 1, 7)]
    back = send(dhs, dh.at[h], pair)
    d_hidden(0)
    for copy in hops:
        copy.wait_recv()
    for k in range(7):
        total += ry[k]
    factor = 1.0 / jnp.sqrt(jnp.sum(total, keepdims=True) / (FF * D) + 1e-06)

    clipped = g[...] * factor
    first = 0.9 * m1v[...] + 0.1 * clipped
    second = 0.95 * m2v[...] + 0.05 * clipped * clipped
    master = mav[...]
    master = master - 0.003 * (first / (jnp.sqrt(second) + 1e-08) + 0.1 * master)
    mine = pl.ds(pl.multiple_of(h * 16, 16), 16)
    ob[z, x, mine, :] = master.astype(BF16)
    swapped = send(ob.at[z, x, mine], ob.at[z, x, mine], pair)
    mav[...] = master
    m1v[...] = first
    m2v[...] = second
    stores = [load(mav, ma_o, 0), load(m1v, m1_o, 4), load(m2v, m2_o, 5)]
    swapped.wait_recv()

    out = Gather(ob)
    out.start()

    def gradients(i):
        cols = pl.ds(i * 128, 128)
        rows = [dh[j % 2, pl.ds((4 * i + j // 2) * 16, 16), :] for j in range(8)]
        dhid = jnp.concatenate(rows, axis=0).T
        gate = gv[:, cols].astype(F32)
        sig = jax.nn.sigmoid(gate)
        ugv[:, cols] = (dhid * (gate * sig)).astype(BF16)
        ggv[:, cols] = (dhid * uv[:, cols].astype(F32) * sig * (1.0 + gate * (1.0 - sig))).astype(BF16)

    out.a_next(0, 0)
    out.a_next(1, 0)
    out.b_next(1)
    out.b_next(2)
    out.a_next(0, 1)
    out.b_next(3)
    out.a_next(1, 1)
    out.b_next(4)
    back.wait_recv()
    for i in range(4):
        gradients(i)
    out.a_next(0, 2)
    for i in range(4, 8):
        gradients(i)
    stores.append(load(ggv, gg_o, 1))
    stores.append(load(ugv, ug_o, 2))
    out.a_next(1, 2)
    out.a_next(0, 3)
    out.a_next(1, 3)
    out.a_next(0, 4)
    out.a_next(1, 4)
    out.finish()
    stores.append(load(ob, w_o, 3))
    for copy in sent:
        copy.wait_send()
    for copy in stores:
        copy.wait()
    assert count[0] == N_COPIES, count[0]


def on_device(*args):
    vm = pltpu.VMEM
    shape = jax.ShapeDtypeStruct
    anywhere = pl.BlockSpec(memory_space=pl.ANY)
    wa, wb = RS_A[0][1], RS_B[0][1]
    *rest, weight = pl.pallas_call(
        kernel,
        out_shape=(
            shape((256, 1024), BF16),
            shape((256, 1024), BF16),
            shape((16, D), F32),
            shape((16, D), F32),
            shape((16, D), F32),
            shape((8, 4, 32, D), BF16),
        ),
        in_specs=[anywhere] * 6,
        out_specs=(anywhere,) * 6,
        scratch_shapes=[
            vm((2, 256, D), BF16),
            vm((256, 1024), BF16),
            vm((256, 1024), BF16),
            vm((16, D), F32),
            vm((16, D), F32),
            vm((16, D), F32),
            vm((8, 4, 16, D), BF16),
            vm((2, 512, 256), BF16),
            vm((512, 256), BF16),
            vm((8, 4, 16, D), F32),
            vm((2, 2, 2, 16, wa), BF16),
            vm((2, 2, 2, 16, wa), BF16),
            vm((2, 2, 3, 4, 16, wa), BF16),
            vm((2, 2, 3, 4, 16, wa), BF16),
            vm((2, 3, 16, wa), BF16),
            vm((2, 3, 16, wa), BF16),
            vm((2, 4, 16, wa), F32),
            vm((2, 3, 8, 16, wb), BF16),
            vm((2, 3, 8, 16, wb), BF16),
            vm((2, 8, 16, wb), F32),
            vm((2, 7, 16, wb), BF16),
            vm((2, 7, 16, wb), BF16),
            vm((16, D), F32),
            vm((3, 8, 128), F32),
            vm((7, 8, 128), F32),
            vm((3, 8, 128), F32),
            vm((7, 8, 128), F32),
            vm((2, 512, 256), F32),
            vm((512, 256), F32),
            vm((8, 4, 32, D), BF16),
            vm((256, 1024), BF16),
            vm((256, 1024), BF16),
            pltpu.SemaphoreType.DMA((N_COPIES,)),
            pltpu.SemaphoreType.DMA((N_COPIES,)),
            pltpu.SemaphoreType.DMA((6,)),
        ],
        compiler_params=pltpu.CompilerParams(
            collective_id=0, has_side_effects=True, vmem_limit_bytes=48 << 20
        ),
        name="step",
    )(*args)
    return (*rest, weight.reshape(1024, D))


def solution(mesh):
    rows = P(("tensor", "dp"), None)
    both = P("dp", "tensor")
    return jax.shard_map(
        on_device,
        mesh=mesh,
        in_specs=(P("dp", None), both, both, rows, rows, rows),
        out_specs=(both, both, rows, rows, rows, P("tensor", None)),
        check_vma=False,
    )
```

time: 1210 us -> 152 us (0.13)
  waiting for transfers between devices: 1100 us -> 0 us
  Pallas kernels: 0 us -> 136 us
  blocking collectives: 73.3 us -> 0 us
  between operations: 14.5 us -> 0.66 us
  matrix products: 13.6 us -> 0 us
    reduce_scatter x1 -> x0, waiting for transfers between devices: 832 us -> none  [on_device(): grad = lax.psum_scatter(partial_term, 'dp', scatter_dimension=0, tiled=True)]
    all_gather x2 -> x0, waiting for transfers between devices: 266 us -> none  [the longest x1 134 us: on_device(): lax.all_gather(weight, 'dp', axis=0, tiled=True)]
    pallas_call x0 -> x1, Pallas kernels: none -> 136 us  [on_device(): pl.pallas_call(kernel, out_shape=(shape((256, 1024), BF16), shape((256, 1...]
    psum x1 -> x0, blocking collectives: 73.3 us -> none  [on_device(): total = lax.psum(local_squares, ('dp', 'tensor'))]
    dot_general x2 -> x0, matrix products: 13.6 us -> none  [the longest x1 7.68 us: on_device(): lax.dot_general(hidden, d_out, (((0,), (0,)), ((), ())), preferred_elemen...]
  transfers between devices with their start and end apart: 3 -> 0, of which waited for: 3 -> 0; matrix products, arithmetic and copies ran while one was open for 0% -> 0% of each run, Pallas kernels for 0% -> 0%
where the time goes in v1:
time: 152 us
  Pallas kernels  136 us (89%)
  local copies, waits for them, and re-layouts  15.8 us (10%)
    pallas_call x1, Pallas kernels, on_device(): pl.pallas_call(kernel, out_shape=(shape((256, 1024), BF16), shape((256, 1...  136 us
    unnamed x18, local copies, waits for them, and re-layouts  15.8 us

profile of v1, /device:TPU:8, one launch (start us, length us, event | category | flops | bytes accessed | tf_op | source)
XLA Modules:
  0.0 152.0 jit_solution(7775116551775688941)
XLA Ops:
  0.6 0.0 copy-start
  0.6 1.4 copy-done
  2.0 0.0 copy-start.1
  2.0 1.0 copy-done.1
  3.1 0.0 copy-start.2
  3.1 1.0 copy-done.2
  4.1 0.0 copy-start.3
  4.1 0.9 copy-done.3
  5.1 0.0 copy-start.4
  5.1 0.9 copy-done.4
  6.0 0.0 copy-start.5
  6.0 0.9 copy-done.5
  6.9 135.5 %step.1 = (bf16[256,1024]{1,0:T(8,128)(2,1)S(1)}, bf16[256,1024]{1,0:T(8,128)(2,1)S(1)}, f32[16,3072]{1,0:T(8,128)S(1)}, f32[16,3072]{1,0:T(8,128)S(1)}, f32[16,...) custom-call(bf16[256,3072]{1,0:T(8,128)(2,1)S(1)} %copy-done, bf16[256,1024]{1,0:T(8,128)(2,1)S(1)} %copy-done.1, ...), custom_call_target="tpu_custom_call" | custom-call | tf_op jit(solution)/shard_map/step/pallas_call | solution.py:400
  142.4 0.8 copy.18
  143.2 0.8 copy.19
  144.0 0.7 copy.20
  144.7 0.7 copy.21
  145.4 0.7 copy.22
  146.1 5.9 %copy.23 = bf16[1024,3072]{1,0:T(8,128)(2,1)} copy(bf16[1024,3072]{1,0:T(8,128)(2,1)} %bitcast.1) | data formatting | bytes 12582912
Async XLA Ops:
  0.6 1.4 copy-start
  2.0 1.0 copy-start.1
  3.1 1.0 copy-start.2
  4.1 0.9 copy-start.3
  5.1 0.9 copy-start.4
  6.0 0.9 copy-start.5

commit v2 on v1

v2 whole, which is shorter than its diff:
```python
import functools

import jax
import jax.numpy as jnp
from jax import lax
from jax.experimental import pallas as pl
from jax.experimental.pallas import tpu as pltpu
from jax.sharding import PartitionSpec as P

D = 3072
FF = 4096
MESH = pl.DeviceIdType.MESH
F32 = jnp.float32
BF16 = jnp.bfloat16

RS_A = ((1024, 768), (2304, 768))
RS_B = ((0, 1024), (1792, 512))
CHUNKS = (RS_B[0], RS_A[0], RS_B[1], RS_A[1])
W_A = ((0, 768), (768, 768))
W_B = (1536, 1536)
N_C = ((0, 640), (640, 640))
N_A = (1280, 640)
N_B = (1920, 1152)
N_SWAP = (1280, 1792)

N_COPIES = (2 * 11 + 32) + 18 + 2 * (8 + 3) + 2 * (3 + 7) + 17 + 1 + 2 * 19 + 11 + 32


def kernel(
    d_in, g_in, u_in, ma_in, m1_in, m2_in,
    ggv, ugv, ma_o, m1_o, m2_o, ob,
    d2, gv, uv, mav, m1v, m2v, wg, ht, hr, gr,
    sah, rah, sa, ra, sax, rax, acca,
    sb0, rb0, accb0, sbz0, rbz0, sb1, rb1, accb1, sbz1, rbz1,
    g, sq, rz, rx, ry, dh, dhs, dhr, dht,
    ssem, rsem, lsem,
):
    dp, tensor = lax.axis_index("dp"), lax.axis_index("tensor")
    z, x, h = dp // 8, (dp // 2) % 4, dp % 2
    yl, c = tensor // 2, tensor % 2
    y = 2 * h + yl

    def device(zz, xx, yy, cc):
        return (zz * 8 + xx * 2 + yy // 2, (yy % 2) * 2 + cc)

    def at_z(k):
        return device((z + k + 8) % 8, x, y, c)

    def at_x(k):
        return device(z, (x + k + 4) % 4, y, c)

    sb, rb, accb, sbz, rbz = (sb0, sb1), (rb0, rb1), (accb0, accb1), (sbz0, sbz1), (rbz0, rbz1)
    across = device(z, x, 3 - y, c)
    beside = device(z, x, 2 * h + 1 - yl, c)
    mate = device(z, x, y, 1 - c)
    pair = (z * 8 + x * 2 + 1 - h, tensor)

    def near(k):
        i = (y * 2 + c + k) % 8
        return device(z, x, i // 2, i % 2)

    count = [0]
    sent = []

    def send(src, dst, to):
        i = count[0]
        count[0] += 1
        copy = pltpu.make_async_remote_copy(
            src_ref=src, dst_ref=dst, send_sem=ssem.at[i], recv_sem=rsem.at[i],
            device_id=to, device_id_type=MESH,
        )
        copy.start()
        sent.append(copy)
        return copy

    def load(src, dst, i):
        copy = pltpu.make_async_copy(src, dst, lsem.at[i])
        copy.start()
        return copy

    load_ma = load(ma_in, mav, 0)
    load_g = load(g_in, gv, 1)
    load_u = load(u_in, uv, 2)
    load_d = load(d_in, d2.at[0], 3)
    load_m1 = load(m1_in, m1v, 4)
    load_m2 = load(m2_in, m2v, 5)

    barrier = pltpu.get_barrier_semaphore()
    friends = (
        [at_z(k) for k in range(1, 8)]
        + [at_x(k) for k in range(1, 4)]
        + [near(k) for k in range(1, 8)]
    )
    for friend in friends:
        pl.semaphore_signal(barrier, inc=1, device_id=friend, device_id_type=MESH)
    load_ma.wait()
    wg[z, x] = mav[...].astype(BF16)
    pl.semaphore_wait(barrier, len(friends))

    class AlongXZ:
        def __init__(self, buf, rows, cols, to_pair=False):
            self.buf, self.rows, self.cols, self.to_pair = buf, rows, pl.ds(*cols), to_pair
            self.paired = []

        def start(self):
            own = self.buf.at[z, x, self.rows, self.cols]
            self.got = [send(own, own, at_x(k)) for k in (1, 3, 2)]

        def forward(self, block):
            if self.to_pair:
                self.paired.append(send(block, block, pair))

        def next(self, s):
            for copy in self.got:
                copy.wait_recv()
            a, b = (pl.ds(0, 4), pl.ds(0, 4)) if s < 3 else (pl.ds(0, 2), pl.ds(2, 2))
            if s < 4:
                up = self.buf.at[(z - s + 8) % 8, a, self.rows, self.cols]
                down = self.buf.at[(z + s) % 8, b, self.rows, self.cols]
                self.got = [send(up, up, at_z(1)), send(down, down, at_z(-1))]
            for k, part in ((-s, pl.ds(0, 4)), (s, pl.ds(0, 4)))[s == 0 :] if s < 4 else ((4, pl.ds(0, 4)),):
                self.forward(self.buf.at[(z + k + 8) % 8, part, self.rows, self.cols])

        def finish(self):
            for copy in self.paired:
                copy.wait_recv()

    class AlongZX:
        def __init__(self, buf, rows, cols):
            self.buf, self.rows, self.cols = buf, rows, cols
            self.spread = []

        def start(self):
            self.along_x(z)
            self.along_z(1)

        def along_x(self, zz):
            block = self.buf.at[zz, x, self.rows, pl.ds(*self.cols)]
            self.spread += [send(block, block, at_x(k)) for k in (1, 3, 2)]

        def along_z(self, s):
            c0, w = self.cols
            a, b = ((c0, w), (c0, w)) if s < 4 else ((c0, w // 2), (c0 + w // 2, w // 2))
            if s == 4 and w % 256:
                a, b = (c0, w // 2 - 64), (c0 + w // 2 - 64, w // 2 + 64)
            up = self.buf.at[(z - s + 9) % 8, x, self.rows, pl.ds(*a)]
            down = self.buf.at[(z + s - 1) % 8, x, self.rows, pl.ds(*b)]
            self.got = [send(up, up, at_z(1)), send(down, down, at_z(-1))]

        def next(self, s):
            for copy in self.got:
                copy.wait_recv()
            if s < 4:
                self.along_z(s + 1)
                self.along_x((z - s + 8) % 8)
                self.along_x((z + s) % 8)
            else:
                self.along_x((z + 4) % 8)

        def finish(self):
            for copy in self.spread:
                copy.wait_recv()

    everything = pl.ds(0, 16)
    w_a = [AlongXZ(wg, everything, cols) for cols in W_A]
    w_b = AlongZX(wg, everything, W_B)
    w_a[0].start()
    w_a[1].start()

    load_d.wait()
    theirs = pl.ds(pl.multiple_of((1 - yl) * 128 + c * 64, 64), 64)
    mine = pl.ds(pl.multiple_of(yl * 128 + c * 64, 64), 64)
    cross, side, swap = [None] * 4, [None] * 4, [[] for _ in range(4)]

    def take(k):
        cols = pl.ds(*CHUNKS[k])
        cross[k] = send(d2.at[0, theirs, cols], d2.at[1, theirs, cols], across)

    def pass_on(k):
        cross[k].wait_recv()
        block = d2.at[1, mine, pl.ds(*CHUNKS[k])]
        side[k] = send(block, block, beside)
        swap[k].append(send(block, block, mate))

    def pass_on_again(k):
        side[k].wait_recv()
        block = d2.at[1, theirs, pl.ds(*CHUNKS[k])]
        swap[k].append(send(block, block, mate))

    take(0)
    take(1)
    w_b.start()

    load_g.wait()
    load_u.wait()
    for i in range(8):
        cols = pl.ds(i * 128, 128)
        gate = gv[:, cols].astype(F32)
        hidden = gate * jax.nn.sigmoid(gate) * uv[:, cols].astype(F32)
        turned = hidden.astype(BF16).astype(F32).T.astype(BF16)
        for j in range(8):
            ht[j % 2, pl.ds((4 * i + j // 2) * 16, 16), :] = turned[j * 16 : j * 16 + 16, :]
    hid = send(ht.at[1 - h], hr, pair)

    take(2)
    take(3)
    w_a[0].next(0)
    w_a[1].next(0)
    pass_on(0)
    w_b.next(1)
    pass_on(1)
    w_b.next(2)
    pass_on_again(0)
    pass_on(2)
    w_a[0].next(1)
    pass_on_again(1)
    pass_on(3)
    w_a[1].next(1)
    hid.wait_recv()

    def partial_sums(k):
        c0, w = CHUNKS[k]
        for copy in swap[k]:
            copy.wait_recv()
        for i in range(w // 256):
            cols = pl.ds(c0 + i * 256, 256)
            acc = jnp.dot(ht[h], d2[0, :, cols], preferred_element_type=F32)
            acc += jnp.dot(hr[...], d2[1, :, cols], preferred_element_type=F32)
            gr[:, :, :, cols] = acc.reshape(8, 4, 16, 256)

    ring = [[[None, None] for _ in range(4)] for _ in RS_A]
    last_x = [None] * 2

    def a_send(j, s):
        cols = pl.ds(*RS_A[j])
        for way, sign in ((0, 1), (1, -1)):
            to = (z + sign * (5 - s) + 8) % 8
            if s == 1:
                part = pl.ds(2 * way, 2)
                sah[j, way] = gr[to, part, :, cols].astype(BF16)
                ring[j][0][way] = send(sah.at[j, way], rah.at[j, way], at_z(sign))
                continue
            ring[j][s - 2][way].wait_recv()
            if s == 2:
                part, rest = pl.ds(2 * way, 2), pl.ds(2 - 2 * way, 2)
                sa[j, way, 0, part] = (gr[to, part, :, cols] + rah[j, way].astype(F32)).astype(BF16)
                sa[j, way, 0, rest] = gr[to, rest, :, cols].astype(BF16)
            else:
                sa[j, way, s - 2] = (gr[to, :, :, cols] + ra[j, way, s - 3].astype(F32)).astype(BF16)
            ring[j][s - 1][way] = send(sa.at[j, way, s - 2], ra.at[j, way, s - 2], at_z(sign))

    def a_turn(j):
        cols = pl.ds(*RS_A[j])
        for way in (0, 1):
            ring[j][3][way].wait_recv()
        acca[j] = gr[z, :, :, cols] + ra[j, 0, 2].astype(F32) + ra[j, 1, 2].astype(F32)
        last_x[j] = []
        for k in (1, 3, 2):
            sax[j, k - 1] = acca[j, (x + k) % 4].astype(BF16)
            last_x[j].append(send(sax.at[j, k - 1], rax.at[j, k - 1], at_x(k)))

    def a_end(j):
        for copy in last_x[j]:
            copy.wait_recv()
        total = acca[j, x]
        for k in range(3):
            total += rax[j, k].astype(F32)
        g[:, pl.ds(*RS_A[j])] = total

    first_x = [None] * 2
    last_z = [None] * 2

    def b_send(j):
        first_x[j] = []
        for k in (1, 3, 2):
            sb[j][k - 1] = gr[:, (x + k) % 4, :, pl.ds(*RS_B[j])].astype(BF16)
            first_x[j].append(send(sb[j].at[k - 1], rb[j].at[k - 1], at_x(k)))

    def b_turn(j):
        for copy in first_x[j]:
            copy.wait_recv()
        total = gr[:, x, :, pl.ds(*RS_B[j])]
        for k in range(3):
            total += rb[j][k].astype(F32)
        accb[j][...] = total
        last_z[j] = []
        for k in (4, 3, 5, 2, 6, 1, 7):
            sbz[j][k - 1] = accb[j][(z + k) % 8].astype(BF16)
            last_z[j].append(send(sbz[j].at[k - 1], rbz[j].at[k - 1], at_z(k)))

    def b_end(j):
        for copy in last_z[j]:
            copy.wait_recv()
        total = accb[j][z]
        for k in range(7):
            total += rbz[j][k].astype(F32)
        g[:, pl.ds(*RS_B[j])] = total

    partial_sums(0)
    b_send(0)
    partial_sums(1)
    a_send(0, 1)
    pass_on_again(2)
    pass_on_again(3)
    w_b.next(3)
    partial_sums(2)
    b_send(1)
    a_send(0, 2)
    partial_sums(3)
    a_send(1, 1)
    a_send(0, 3)
    a_send(1, 2)
    b_turn(0)
    a_send(0, 4)
    a_send(1, 3)
    b_turn(1)
    a_turn(0)
    a_send(1, 4)
    w_b.next(4)
    w_a[0].next(2)
    a_turn(1)
    w_a[1].next(2)
    b_end(0)
    a_end(0)
    b_end(1)
    a_end(1)

    square = g[...] * g[...]
    square = square[:8] + square[8:]
    total = square[:, 0:128]
    for i in range(1, 24):
        total += square[:, i * 128 : i * 128 + 128]
    sq[0] = total
    load_m1.wait()
    load_m2.wait()
    hops = [send(sq.at[0], rz.at[k - 1], at_z(k)) for k in (4, 3, 5, 2, 6, 1, 7)]

    def d_hidden(j):
        acc = None
        for i in range(6):
            cols = pl.ds(i * 512, 512)
            part = lax.dot_general(
                wg[:, :, :, cols].reshape(512, 512), d2[j, :, cols],
                (((1,), (1,)), ((), ())), preferred_element_type=F32,
            )
            acc = part if acc is None else acc + part
        if j == 0:
            dh[...] = acc
        else:
            dhs[...] = acc.astype(BF16)

    w_a[0].next(3)
    w_a[1].next(3)
    for copy in hops:
        copy.wait_recv()
    for k in range(7):
        total += rz[k]
    sq[1] = total
    hops = [send(sq.at[1], rx.at[k - 1], at_x(k)) for k in (2, 1, 3)]
    w_a[0].next(4)
    w_a[1].next(4)
    for copy in hops:
        copy.wait_recv()
    for k in range(3):
        total += rx[k]
    sq[2] = total
    hops = [send(sq.at[2], ry.at[k - 1], near(k)) for k in (4, 3, 5, 2, 6, 1, 7)]
    w_b.finish()
    d_hidden(1)
    back = send(dhs, dhr, pair)
    for copy in hops:
        copy.wait_recv()
    for k in range(7):
        total += ry[k]
    factor = 1.0 / jnp.sqrt(jnp.sum(total, keepdims=True) / (FF * D) + 1e-06)

    clipped = g[...] * factor
    first = 0.9 * m1v[...] + 0.1 * clipped
    second = 0.95 * m2v[...] + 0.05 * clipped * clipped
    master = mav[...]
    master = master - 0.003 * (first / (jnp.sqrt(second) + 1e-08) + 0.1 * master)
    own = pl.ds(pl.multiple_of(h * 16, 16), 16)
    ob[z, x, own, :] = master.astype(BF16)

    n_c = [AlongXZ(ob, own, cols, to_pair=True) for cols in N_C]
    n_a = AlongXZ(ob, pl.ds(0, 32), N_A)
    n_b = AlongZX(ob, pl.ds(0, 32), N_B)
    block = ob.at[z, x, own, pl.ds(*N_SWAP)]
    n_c[0].start()
    swapped = send(block, block, pair)
    n_c[1].start()
    ma_o[...] = master
    m1_o[...] = first
    m2_o[...] = second

    def gradients(i):
        cols = pl.ds(i * 128, 128)
        rows = [dht[j % 2, pl.ds((4 * i + j // 2) * 16, 16), :] for j in range(8)]
        dhid = jnp.concatenate(rows, axis=0).T
        gate = gv[:, cols].astype(F32)
        sig = jax.nn.sigmoid(gate)
        ugv[:, cols] = (dhid * (gate * sig)).astype(BF16)
        ggv[:, cols] = (dhid * uv[:, cols].astype(F32) * sig * (1.0 + gate * (1.0 - sig))).astype(BF16)

    n_c[0].next(0)
    n_c[1].next(0)
    swapped.wait_recv()
    n_a.start()
    n_b.start()
    d_hidden(0)
    n_c[0].next(1)
    n_c[1].next(1)
    n_b.next(1)
    n_a.next(0)
    n_b.next(2)
    n_c[0].next(2)
    n_c[1].next(2)
    n_b.next(3)
    n_a.next(1)
    n_b.next(4)
    n_c[0].next(3)
    n_c[1].next(3)
    n_a.next(2)
    back.wait_recv()
    dht[h] = dh[...]
    dht[1 - h] = dhr[...].astype(F32)
    for i in range(4):
        gradients(i)
    n_c[0].next(4)
    n_c[1].next(4)
    n_a.next(3)
    for i in range(4, 8):
        gradients(i)
    n_a.next(4)
    n_b.finish()
    n_c[0].finish()
    n_c[1].finish()
    for copy in sent:
        copy.wait_send()
    assert count[0] == N_COPIES, (count[0], N_COPIES)


def store(*refs):
    sem = refs[-1]
    copies = [pltpu.make_async_copy(refs[i], refs[6 + i], sem.at[i]) for i in (5, 0, 1, 2, 3, 4)]
    for copy in copies:
        copy.start()
    for copy in copies:
        copy.wait()


def on_device(*args):
    vm = pltpu.VMEM
    shape = jax.ShapeDtypeStruct
    inside = pl.BlockSpec(memory_space=pltpu.VMEM)
    outside = pl.BlockSpec(memory_space=pltpu.HBM)
    wa = RS_A[0][1]
    shapes = (
        ((256, 1024), BF16), ((256, 1024), BF16), ((16, D), F32), ((16, D), F32), ((16, D), F32), ((8, 4, 32, D), BF16)
    )
    results = pl.pallas_call(
        kernel,
        out_shape=tuple(vm(*leaf) for leaf in shapes),
        in_specs=[outside] * 6,
        out_specs=(inside,) * 6,
        scratch_shapes=[
            vm((2, 256, D), BF16),
            vm((256, 1024), BF16),
            vm((256, 1024), BF16),
            vm((16, D), F32),
            vm((16, D), F32),
            vm((16, D), F32),
            vm((8, 4, 16, D), BF16),
            vm((2, 512, 256), BF16),
            vm((512, 256), BF16),
            vm((8, 4, 16, D), F32),
            vm((2, 2, 2, 16, wa), BF16),
            vm((2, 2, 2, 16, wa), BF16),
            vm((2, 2, 3, 4, 16, wa), BF16),
            vm((2, 2, 3, 4, 16, wa), BF16),
            vm((2, 3, 16, wa), BF16),
            vm((2, 3, 16, wa), BF16),
            vm((2, 4, 16, wa), F32),
            *(
                vm(leaf, kind)
                for _, wb in RS_B
                for leaf, kind in (
                    ((3, 8, 16, wb), BF16), ((3, 8, 16, wb), BF16), ((8, 16, wb), F32),
                    ((7, 16, wb), BF16), ((7, 16, wb), BF16),
                )
            ),
            vm((16, D), F32),
            vm((3, 8, 128), F32),
            vm((7, 8, 128), F32),
            vm((3, 8, 128), F32),
            vm((7, 8, 128), F32),
            vm((512, 256), F32),
            vm((512, 256), BF16),
            vm((512, 256), BF16),
            vm((2, 512, 256), F32),
            pltpu.SemaphoreType.DMA((N_COPIES,)),
            pltpu.SemaphoreType.DMA((N_COPIES,)),
            pltpu.SemaphoreType.DMA((6,)),
        ],
        compiler_params=pltpu.CompilerParams(
            collective_id=0, has_side_effects=True, vmem_limit_bytes=48 << 20
        ),
        name="step",
    )(*args)
    *rest, weight = pl.pallas_call(
        store,
        out_shape=tuple(shape(*leaf) for leaf in shapes),
        in_specs=[inside] * 6,
        out_specs=(outside,) * 6,
        scratch_shapes=[pltpu.SemaphoreType.DMA((6,))],
        compiler_params=pltpu.CompilerParams(vmem_limit_bytes=1 << 20),
        name="store",
    )(*(pltpu.with_memory_space_constraint(leaf, pltpu.VMEM) for leaf in results))
    return (*rest, weight.reshape(1024, D))


def solution(mesh):
    rows = P(("tensor", "dp"), None)
    both = P("dp", "tensor")
    return jax.shard_map(
        on_device,
        mesh=mesh,
        in_specs=(P("dp", None), both, both, rows, rows, rows),
        out_specs=(both, both, rows, rows, rows, P("tensor", None)),
        check_vma=False,
    )
```

time: 152 us -> 121 us (0.80)
  Pallas kernels: 136 us -> 119 us
  local copies, waits for them, and re-layouts: 15.8 us -> 0 us
    pallas_call x1 -> x2, Pallas kernels: 136 us -> 119 us  [the longest x1 116 us: on_device(): pl.pallas_call(kernel, out_shape=tuple((vm(*leaf) for leaf in shapes)), i...]
    unnamed x18 -> x0, local copies, waits for them, and re-layouts: 15.8 us -> none
where the time goes in v2:
time: 121 us; the launch traced here: 120 us
  Pallas kernels  119 us (98%)
    pallas_call x1, Pallas kernels, on_device(): pl.pallas_call(kernel, out_shape=tuple((vm(*leaf) for leaf in shapes)), i...  116 us
    pallas_call x1, Pallas kernels, on_device(): pl.pallas_call(store, out_shape=tuple((shape(*leaf) for leaf in shapes)),...  3.24 us

profile of v2, /device:TPU:8, one launch (start us, length us, event | category | flops | bytes accessed | tf_op | source)
XLA Modules:
  0.0 120.1 jit_solution(1270481944419763841)
XLA Ops:
  0.6 116.2 %step.1 = (bf16[256,1024]{1,0:T(8,128)(2,1)S(1)}, bf16[256,1024]{1,0:T(8,128)(2,1)S(1)}, f32[16,3072]{1,0:T(8,128)S(1)}, f32[16,3072]{1,0:T(8,128)S(1)}, f32[16,...) custom-call(bf16[256,3072]{1,0:T(8,128)(2,1)} %d_in.1, bf16[256,1024]{1,0:T(8,128)(2,1)} %g_in.1, ...), custom_call_target="tpu_custom_call" | custom-call | tf_op jit(solution)/shard_map/step/pallas_call | solution.py:461
  116.8 3.2 %store.1 = (bf16[256,1024]{1,0:T(8,128)(2,1)}, bf16[256,1024]{1,0:T(8,128)(2,1)}, f32[16,3072]{1,0:T(8,128)}, f32[16,3072]{1,0:T(8,128)}, f32[16,3072]{1,0:T(8,128)}, /*index=5*/bf16[8,4,32,3072]{3,2,1,0:T(8,128)(2,1)}) custom-call(bf16[256,1024]{1,0:T(8,128)(2,1)S(1)} %get-tuple-element.18.refs_0_, bf16[256,1024]{1,0:T(8,128)(2,1)S(1)} %get-tuple-element.19.refs_1_, ...), custom_call_target="tpu_custom_call" | custom-call | tf_op jit(solution)/shard_map/store/pallas_call | solution.py:510

commit v3 on v2

--- a/solution.py
+++ b/solution.py
@@ -23,7 +23,7 @@
 N_B = (1920, 1152)
 N_SWAP = (1280, 1792)
 
-N_COPIES = (2 * 11 + 32) + 18 + 2 * (8 + 3) + 2 * (3 + 7) + 17 + 1 + 2 * 19 + 11 + 32
+N_COPIES = (2 * 11 + 32) + 18 + 2 * (8 + 3) + 2 * (3 + 7) + 17 + 1 + 2 * 19 + 11 + 2 * 32
 
 
 def kernel(
@@ -164,15 +164,13 @@
     everything = pl.ds(0, 16)
     w_a = [AlongXZ(wg, everything, cols) for cols in W_A]
     w_b = AlongZX(wg, everything, W_B)
-    w_a[0].start()
-    w_a[1].start()
-
-    load_d.wait()
     theirs = pl.ds(pl.multiple_of((1 - yl) * 128 + c * 64, 64), 64)
     mine = pl.ds(pl.multiple_of(yl * 128 + c * 64, 64), 64)
     cross, side, swap = [None] * 4, [None] * 4, [[] for _ in range(4)]
 
     def take(k):
+        if k == 0:
+            load_d.wait()
         cols = pl.ds(*CHUNKS[k])
         cross[k] = send(d2.at[0, theirs, cols], d2.at[1, theirs, cols], across)
 
@@ -187,39 +185,24 @@
         block = d2.at[1, theirs, pl.ds(*CHUNKS[k])]
         swap[k].append(send(block, block, mate))
 
-    take(0)
-    take(1)
-    w_b.start()
-
-    load_g.wait()
-    load_u.wait()
-    for i in range(8):
-        cols = pl.ds(i * 128, 128)
-        gate = gv[:, cols].astype(F32)
-        hidden = gate * jax.nn.sigmoid(gate) * uv[:, cols].astype(F32)
-        turned = hidden.astype(BF16).astype(F32).T.astype(BF16)
-        for j in range(8):
-            ht[j % 2, pl.ds((4 * i + j // 2) * 16, 16), :] = turned[j * 16 : j * 16 + 16, :]
-    hid = send(ht.at[1 - h], hr, pair)
-
-    take(2)
-    take(3)
-    w_a[0].next(0)
-    w_a[1].next(0)
-    pass_on(0)
-    w_b.next(1)
-    pass_on(1)
-    w_b.next(2)
-    pass_on_again(0)
-    pass_on(2)
-    w_a[0].next(1)
-    pass_on_again(1)
-    pass_on(3)
-    w_a[1].next(1)
-    hid.wait_recv()
+    hid = []
+
+    def hide():
+        load_g.wait()
+        load_u.wait()
+        for i in range(8):
+            cols = pl.ds(i * 128, 128)
+            gate = gv[:, cols].astype(F32)
+            hidden = gate * jax.nn.sigmoid(gate) * uv[:, cols].astype(F32)
+            turned = hidden.astype(BF16).astype(F32).T.astype(BF16)
+            for j in range(8):
+                ht[j % 2, pl.ds((4 * i + j // 2) * 16, 16), :] = turned[j * 16 : j * 16 + 16, :]
+        hid.append(send(ht.at[1 - h], hr, pair))
 
     def partial_sums(k):
         c0, w = CHUNKS[k]
+        if k == 0:
+            hid[0].wait_recv()
         for copy in swap[k]:
             copy.wait_recv()
         for i in range(w // 256):
@@ -296,46 +279,41 @@
             total += rbz[j][k].astype(F32)
         g[:, pl.ds(*RS_B[j])] = total
 
-    partial_sums(0)
-    b_send(0)
-    partial_sums(1)
-    a_send(0, 1)
-    pass_on_again(2)
-    pass_on_again(3)
-    w_b.next(3)
-    partial_sums(2)
-    b_send(1)
-    a_send(0, 2)
-    partial_sums(3)
-    a_send(1, 1)
-    a_send(0, 3)
-    a_send(1, 2)
-    b_turn(0)
-    a_send(0, 4)
-    a_send(1, 3)
-    b_turn(1)
-    a_turn(0)
-    a_send(1, 4)
-    w_b.next(4)
-    w_a[0].next(2)
-    a_turn(1)
-    w_a[1].next(2)
-    b_end(0)
-    a_end(0)
-    b_end(1)
-    a_end(1)
-
-    square = g[...] * g[...]
-    square = square[:8] + square[8:]
-    total = square[:, 0:128]
-    for i in range(1, 24):
-        total += square[:, i * 128 : i * 128 + 128]
-    sq[0] = total
-    load_m1.wait()
-    load_m2.wait()
-    hops = [send(sq.at[0], rz.at[k - 1], at_z(k)) for k in (4, 3, 5, 2, 6, 1, 7)]
+    rounds = []
+
+    def exchange(i, dst, hops):
+        rounds.append([send(sq.at[i], dst.at[k - 1], to(k)) for k, to in hops])
+
+    def arrived(i, dst, n):
+        for copy in rounds[i]:
+            copy.wait_recv()
+        total = sq[i]
+        for k in range(n):
+            total += dst[k]
+        return total
+
+    def squares():
+        square = g[...] * g[...]
+        square = square[:8] + square[8:]
+        total = square[:, 0:128]
+        for i in range(1, 24):
+            total += square[:, i * 128 : i * 128 + 128]
+        sq[0] = total
+        exchange(0, rz, [(k, at_z) for k in (4, 3, 5, 2, 6, 1, 7)])
+
+    def squares_x():
+        sq[1] = arrived(0, rz, 7)
+        exchange(1, rx, [(k, at_x) for k in (2, 1, 3)])
+
+    def squares_y():
+        sq[2] = arrived(1, rx, 3)
+        exchange(2, ry, [(k, near) for k in (4, 3, 5, 2, 6, 1, 7)])
+
+    back = []
 
     def d_hidden(j):
+        if j == 1:
+            w_b.finish()
         acc = None
         for i in range(6):
             cols = pl.ds(i * 512, 512)
@@ -348,50 +326,42 @@
             dh[...] = acc
         else:
             dhs[...] = acc.astype(BF16)
-
-    w_a[0].next(3)
-    w_a[1].next(3)
-    for copy in hops:
-        copy.wait_recv()
-    for k in range(7):
-        total += rz[k]
-    sq[1] = total
-    hops = [send(sq.at[1], rx.at[k - 1], at_x(k)) for k in (2, 1, 3)]
-    w_a[0].next(4)
-    w_a[1].next(4)
-    for copy in hops:
-        copy.wait_recv()
-    for k in range(3):
-        total += rx[k]
-    sq[2] = total
-    hops = [send(sq.at[2], ry.at[k - 1], near(k)) for k in (4, 3, 5, 2, 6, 1, 7)]
-    w_b.finish()
-    d_hidden(1)
-    back = send(dhs, dhr, pair)
-    for copy in hops:
-        copy.wait_recv()
-    for k in range(7):
-        total += ry[k]
-    factor = 1.0 / jnp.sqrt(jnp.sum(total, keepdims=True) / (FF * D) + 1e-06)
-
-    clipped = g[...] * factor
-    first = 0.9 * m1v[...] + 0.1 * clipped
-    second = 0.95 * m2v[...] + 0.05 * clipped * clipped
-    master = mav[...]
-    master = master - 0.003 * (first / (jnp.sqrt(second) + 1e-08) + 0.1 * master)
-    own = pl.ds(pl.multiple_of(h * 16, 16), 16)
-    ob[z, x, own, :] = master.astype(BF16)
+            back.append(send(dhs, dhr, pair))
+
+    own, other = (pl.ds(pl.multiple_of(i * 16, 16), 16) for i in (h, 1 - h))
+
+    def adam():
+        load_m1.wait()
+        load_m2.wait()
+        total = arrived(2, ry, 7)
+        factor = 1.0 / jnp.sqrt(jnp.sum(total, keepdims=True) / (FF * D) + 1e-06)
+        clipped = g[...] * factor
+        first = 0.9 * m1v[...] + 0.1 * clipped
+        second = 0.95 * m2v[...] + 0.05 * clipped * clipped
+        master = mav[...]
+        master = master - 0.003 * (first / (jnp.sqrt(second) + 1e-08) + 0.1 * master)
+        ob[z, x, own, :] = master.astype(BF16)
+        ma_o[...] = master
+        m1_o[...] = first
+        m2_o[...] = second
 
     n_c = [AlongXZ(ob, own, cols, to_pair=True) for cols in N_C]
     n_a = AlongXZ(ob, pl.ds(0, 32), N_A)
-    n_b = AlongZX(ob, pl.ds(0, 32), N_B)
-    block = ob.at[z, x, own, pl.ds(*N_SWAP)]
-    n_c[0].start()
-    swapped = send(block, block, pair)
-    n_c[1].start()
-    ma_o[...] = master
-    m1_o[...] = first
-    m2_o[...] = second
+    n_b = [AlongZX(ob, rows, N_B) for rows in (own, other)]
+    swapped = []
+
+    def swap_rows():
+        block = ob.at[z, x, own, pl.ds(*N_SWAP)]
+        swapped.append(send(block, block, pair))
+
+    def swapped_rows():
+        swapped[0].wait_recv()
+        n_a.start()
+
+    def turn_back():
+        back[0].wait_recv()
+        dht[h] = dh[...]
+        dht[1 - h] = dhr[...].astype(F32)
 
     def gradients(i):
         cols = pl.ds(i * 128, 128)
@@ -402,39 +372,104 @@
         ugv[:, cols] = (dhid * (gate * sig)).astype(BF16)
         ggv[:, cols] = (dhid * uv[:, cols].astype(F32) * sig * (1.0 + gate * (1.0 - sig))).astype(BF16)
 
+    take(0)
+    w_b.start()
+    hide()
+    w_a[1].start()
+    w_a[0].start()
+    w_a[0].next(0)
+    take(1)
+    w_b.next(1)
+    take(2)
+    take(3)
+    pass_on(0)
+    w_a[1].next(0)
+    w_a[0].next(1)
+    pass_on(1)
+    w_b.next(2)
+    pass_on_again(0)
+    w_a[1].next(1)
+    pass_on(3)
+    pass_on_again(1)
+    partial_sums(0)
+    b_send(0)
+    pass_on(2)
+    partial_sums(1)
+    a_send(0, 1)
+    pass_on_again(3)
+    w_a[0].next(2)
+    a_send(0, 2)
+    pass_on_again(2)
+    partial_sums(3)
+    a_send(1, 1)
+    partial_sums(2)
+    a_send(0, 3)
+    b_send(1)
+    a_send(1, 2)
+    a_send(0, 4)
+    a_send(1, 3)
+    b_turn(0)
+    a_send(1, 4)
+    b_turn(1)
+    w_b.next(3)
+    a_turn(0)
+    a_turn(1)
+    w_a[0].next(3)
+    b_end(0)
+    b_end(1)
+    w_b.next(4)
+    a_end(1)
+    a_end(0)
+    squares()
+    w_a[1].next(2)
+    squares_x()
+    w_a[0].next(4)
+    w_a[1].next(3)
+    squares_y()
+    adam()
+    swap_rows()
+    w_a[1].next(4)
+    n_c[0].start()
+    n_b[0].start()
+    d_hidden(1)
+    n_c[1].start()
+    n_b[0].next(1)
+    swapped_rows()
     n_c[0].next(0)
+    n_b[1].start()
     n_c[1].next(0)
-    swapped.wait_recv()
-    n_a.start()
-    n_b.start()
+    n_b[0].next(2)
     d_hidden(0)
     n_c[0].next(1)
+    n_b[1].next(1)
     n_c[1].next(1)
-    n_b.next(1)
+    n_b[0].next(3)
     n_a.next(0)
-    n_b.next(2)
+    n_b[1].next(2)
+    n_c[1].next(2)
     n_c[0].next(2)
-    n_c[1].next(2)
-    n_b.next(3)
+    n_b[0].next(4)
+    n_b[1].next(3)
     n_a.next(1)
-    n_b.next(4)
+    n_c[1].next(3)
+    turn_back()
+    gradients(0)
     n_c[0].next(3)
-    n_c[1].next(3)
     n_a.next(2)
-    back.wait_recv()
-    dht[h] = dh[...]
-    dht[1 - h] = dhr[...].astype(F32)
-    for i in range(4):
-        gradients(i)
+    n_b[1].next(4)
+    gradients(1)
     n_c[0].next(4)
+    gradients(2)
     n_c[1].next(4)
+    gradients(3)
     n_a.next(3)
-    for i in range(4, 8):
-        gradients(i)
+    gradients(4)
+    gradients(5)
+    gradients(6)
+    gradients(7)
     n_a.next(4)
-    n_b.finish()
-    n_c[0].finish()
-    n_c[1].finish()
+    for part in (*n_b, *n_c):
+        part.finish()
     for copy in sent:
         copy.wait_send()
     assert count[0] == N_COPIES, (count[0], N_COPIES)
@@ -442,7 +477,8 @@
 
 def store(*refs):
     sem = refs[-1]
-    copies = [pltpu.make_async_copy(refs[i], refs[6 + i], sem.at[i]) for i in (5, 0, 1, 2, 3, 4)]
+    pairs = [(refs[5].at[i], refs[11].at[i]) for i in range(8)] + [(refs[i], refs[6 + i]) for i in range(5)]
+    copies = [pltpu.make_async_copy(src, dst, sem.at[i]) for i, (src, dst) in enumerate(pairs)]
     for copy in copies:
         copy.start()
     for copy in copies:
@@ -512,7 +548,7 @@
         out_shape=tuple(shape(*leaf) for leaf in shapes),
         in_specs=[inside] * 6,
         out_specs=(outside,) * 6,
-        scratch_shapes=[pltpu.SemaphoreType.DMA((6,))],
+        scratch_shapes=[pltpu.SemaphoreType.DMA((13,))],
         compiler_params=pltpu.CompilerParams(vmem_limit_bytes=1 << 20),
         name="store",
     )(*(pltpu.with_memory_space_constraint(leaf, pltpu.VMEM) for leaf in results))

time: 121 us -> 120 us (level)
    pallas_call x1, Pallas kernels: 116 us -> 115 us  [on_device(): pl.pallas_call(kernel, out_shape=tuple((vm(*leaf) for leaf in shapes)), i...]
where the time goes in v3:
time: 120 us; the launch traced here: 119 us
  Pallas kernels  118 us (98%)
    pallas_call x1, Pallas kernels, on_device(): pl.pallas_call(kernel, out_shape=tuple((vm(*leaf) for leaf in shapes)), i...  115 us
    pallas_call x1, Pallas kernels, on_device(): pl.pallas_call(store, out_shape=tuple((shape(*leaf) for leaf in shapes)),...  3.25 us

profile of v3, /device:TPU:8, one launch (start us, length us, event | category | flops | bytes accessed | tf_op | source)
XLA Modules:
  0.0 118.7 jit_solution(2320889676925321903)
XLA Ops:
  0.6 114.8 %step.1 = (bf16[256,1024]{1,0:T(8,128)(2,1)S(1)}, bf16[256,1024]{1,0:T(8,128)(2,1)S(1)}, f32[16,3072]{1,0:T(8,128)S(1)}, f32[16,3072]{1,0:T(8,128)S(1)}, f32[16,...) custom-call(bf16[256,3072]{1,0:T(8,128)(2,1)} %d_in.1, bf16[256,1024]{1,0:T(8,128)(2,1)} %g_in.1, ...), custom_call_target="tpu_custom_call" | custom-call | tf_op jit(solution)/shard_map/step/pallas_call | solution.py:497
  115.5 3.3 %store.1 = (bf16[256,1024]{1,0:T(8,128)(2,1)}, bf16[256,1024]{1,0:T(8,128)(2,1)}, f32[16,3072]{1,0:T(8,128)}, f32[16,3072]{1,0:T(8,128)}, f32[16,3072]{1,0:T(8,128)}, /*index=5*/bf16[8,4,32,3072]{3,2,1,0:T(8,128)(2,1)}) custom-call(bf16[256,1024]{1,0:T(8,128)(2,1)S(1)} %get-tuple-element.18.refs_0_, bf16[256,1024]{1,0:T(8,128)(2,1)S(1)} %get-tuple-element.19.refs_1_, ...), custom_call_target="tpu_custom_call" | custom-call | tf_op jit(solution)/shard_map/store/pallas_call | solution.py:546

commit v4 on v3

--- a/solution.py
+++ b/solution.py
@@ -16,12 +16,12 @@
 RS_A = ((1024, 768), (2304, 768))
 RS_B = ((0, 1024), (1792, 512))
 CHUNKS = (RS_B[0], RS_A[0], RS_B[1], RS_A[1])
-W_A = ((0, 768), (768, 768))
-W_B = (1536, 1536)
-N_C = ((0, 640), (640, 640))
-N_A = (1280, 640)
-N_B = (1920, 1152)
-N_SWAP = (1280, 1792)
+W_A = ((0, 768), (768, 640))
+W_B = (1408, 1664)
+N_C = ((0, 256), (256, 896))
+N_A = (1152, 512)
+N_B = (1664, 1408)
+N_SWAP = (1152, 1920)
 
 N_COPIES = (2 * 11 + 32) + 18 + 2 * (8 + 3) + 2 * (3 + 7) + 17 + 1 + 2 * 19 + 11 + 2 * 32
 
@@ -372,102 +372,102 @@
         ugv[:, cols] = (dhid * (gate * sig)).astype(BF16)
         ggv[:, cols] = (dhid * uv[:, cols].astype(F32) * sig * (1.0 + gate * (1.0 - sig))).astype(BF16)
 
+    w_a[1].start()
     take(0)
     w_b.start()
+    w_a[0].start()
     hide()
-    w_a[1].start()
-    w_a[0].start()
     w_a[0].next(0)
+    w_a[1].next(0)
     take(1)
+    pass_on(0)
     w_b.next(1)
     take(2)
+    w_a[0].next(1)
     take(3)
-    pass_on(0)
-    w_a[1].next(0)
-    w_a[0].next(1)
+    w_a[1].next(1)
     pass_on(1)
+    pass_on_again(0)
     w_b.next(2)
-    pass_on_again(0)
-    w_a[1].next(1)
+    partial_sums(0)
     pass_on(3)
+    w_a[0].next(2)
+    b_send(0)
     pass_on_again(1)
-    partial_sums(0)
-    b_send(0)
-    pass_on(2)
+    pass_on_again(3)
     partial_sums(1)
     a_send(0, 1)
-    pass_on_again(3)
-    w_a[0].next(2)
-    a_send(0, 2)
-    pass_on_again(2)
+    w_b.next(3)
     partial_sums(3)
     a_send(1, 1)
+    a_send(0, 2)
+    pass_on(2)
+    a_send(1, 2)
+    pass_on_again(2)
+    a_send(0, 3)
+    a_send(1, 3)
     partial_sums(2)
-    a_send(0, 3)
+    b_turn(0)
+    a_send(0, 4)
     b_send(1)
-    a_send(1, 2)
-    a_send(0, 4)
-    a_send(1, 3)
-    b_turn(0)
+    w_b.next(4)
     a_send(1, 4)
     b_turn(1)
-    w_b.next(3)
+    b_end(0)
+    w_a[1].next(2)
+    w_a[0].next(3)
     a_turn(0)
     a_turn(1)
-    w_a[0].next(3)
-    b_end(0)
+    a_end(0)
     b_end(1)
-    w_b.next(4)
     a_end(1)
-    a_end(0)
     squares()
-    w_a[1].next(2)
     squares_x()
-    w_a[0].next(4)
     w_a[1].next(3)
     squares_y()
     adam()
+    w_a[1].next(4)
     swap_rows()
-    w_a[1].next(4)
+    w_a[0].next(4)
+    n_c[1].start()
+    n_b[0].start()
     n_c[0].start()
-    n_b[0].start()
     d_hidden(1)
-    n_c[1].start()
     n_b[0].next(1)
+    n_c[1].next(0)
+    n_c[0].next(0)
     swapped_rows()
-    n_c[0].next(0)
     n_b[1].start()
-    n_c[1].next(0)
+    d_hidden(0)
+    n_c[1].next(1)
     n_b[0].next(2)
-    d_hidden(0)
+    n_b[1].next(1)
     n_c[0].next(1)
-    n_b[1].next(1)
-    n_c[1].next(1)
+    n_a.next(0)
+    n_c[1].next(2)
+    n_b[1].next(2)
+    n_c[0].next(2)
     n_b[0].next(3)
-    n_a.next(0)
-    n_b[1].next(2)
-    n_c[1].next(2)
-    n_c[0].next(2)
-    n_b[0].next(4)
-    n_b[1].next(3)
     n_a.next(1)
     n_c[1].next(3)
     turn_back()
+    n_b[1].next(3)
+    n_a.next(2)
     gradients(0)
+    n_c[1].next(4)
+    gradients(1)
     n_c[0].next(3)
-    n_a.next(2)
     n_b[1].next(4)
-    gradients(1)
+    gradients(2)
+    n_b[0].next(4)
+    n_a.next(3)
+    gradients(3)
+    gradients(4)
     n_c[0].next(4)
-    gradients(2)
-    n_c[1].next(4)
-    gradients(3)
-    n_a.next(3)
-    gradients(4)
     gradients(5)
     gradients(6)
+    n_a.next(4)
     gradients(7)
-    n_a.next(4)
     for part in (*n_b, *n_c):
         part.finish()
     for copy in sent:

time: 120 us -> 119 us (level)
  no operation moved by 1% of the time
where the time goes in v4:
time: 119 us; the launch traced here: 118 us
  Pallas kernels  118 us (99%)
    pallas_call x1, Pallas kernels, on_device(): pl.pallas_call(kernel, out_shape=tuple((vm(*leaf) for leaf in shapes)), i...  114 us
    pallas_call x1, Pallas kernels, on_device(): pl.pallas_call(store, out_shape=tuple((shape(*leaf) for leaf in shapes)),...  3.25 us

profile of v4, /device:TPU:8, one launch (start us, length us, event | category | flops | bytes accessed | tf_op | source)
XLA Modules:
  0.0 118.4 jit_solution(6986915095894806965)
XLA Ops:
  0.6 114.5 %step.1 = (bf16[256,1024]{1,0:T(8,128)(2,1)S(1)}, bf16[256,1024]{1,0:T(8,128)(2,1)S(1)}, f32[16,3072]{1,0:T(8,128)S(1)}, f32[16,3072]{1,0:T(8,128)S(1)}, f32[16,...) custom-call(bf16[256,3072]{1,0:T(8,128)(2,1)} %d_in.1, bf16[256,1024]{1,0:T(8,128)(2,1)} %g_in.1, ...), custom_call_target="tpu_custom_call" | custom-call | tf_op jit(solution)/shard_map/step/pallas_call | solution.py:497
  115.1 3.3 %store.1 = (bf16[256,1024]{1,0:T(8,128)(2,1)}, bf16[256,1024]{1,0:T(8,128)(2,1)}, f32[16,3072]{1,0:T(8,128)}, f32[16,3072]{1,0:T(8,128)}, f32[16,3072]{1,0:T(8,128)}, /*index=5*/bf16[8,4,32,3072]{3,2,1,0:T(8,128)(2,1)}) custom-call(bf16[256,1024]{1,0:T(8,128)(2,1)S(1)} %get-tuple-element.18.refs_0_, bf16[256,1024]{1,0:T(8,128)(2,1)S(1)} %get-tuple-element.19.refs_1_, ...), custom_call_target="tpu_custom_call" | custom-call | tf_op jit(solution)/shard_map/store/pallas_call | solution.py:546

commit v5 on v4

--- a/solution.py
+++ b/solution.py
@@ -13,17 +13,17 @@
 F32 = jnp.float32
 BF16 = jnp.bfloat16
 
-RS_A = ((1024, 768), (2304, 768))
-RS_B = ((0, 1024), (1792, 512))
+RS_A = ((768, 768), (2304, 768))
+RS_B = ((0, 768), (1536, 768))
 CHUNKS = (RS_B[0], RS_A[0], RS_B[1], RS_A[1])
-W_A = ((0, 768), (768, 640))
-W_B = (1408, 1664)
-N_C = ((0, 256), (256, 896))
-N_A = (1152, 512)
-N_B = (1664, 1408)
-N_SWAP = (1152, 1920)
-
-N_COPIES = (2 * 11 + 32) + 18 + 2 * (8 + 3) + 2 * (3 + 7) + 17 + 1 + 2 * 19 + 11 + 2 * 32
+W_A = ((0, 128), (128, 128))
+W_B = (256, 2816)
+N_C = ((0, 384), (384, 640))
+N_A = (1024, 384)
+N_B = (1408, 1664)
+N_SWAP = (1024, 2048)
+
+N_COPIES = (2 * 11 + 40) + 18 + 2 * (8 + 3) + 2 * (4 + 7) + 17 + 1 + 2 * 19 + 11 + 2 * 40
 
 
 def kernel(
@@ -31,7 +31,7 @@
     ggv, ugv, ma_o, m1_o, m2_o, ob,
     d2, gv, uv, mav, m1v, m2v, wg, ht, hr, gr,
     sah, rah, sa, ra, sax, rax, acca,
-    sb0, rb0, accb0, sbz0, rbz0, sb1, rb1, accb1, sbz1, rbz1,
+    sb0, rb0, sc0, rc0, accb0, sbz0, rbz0, sb1, rb1, sc1, rc1, accb1, sbz1, rbz1,
     g, sq, rz, rx, ry, dh, dhs, dhr, dht,
     ssem, rsem, lsem,
 ):
@@ -49,7 +49,8 @@
     def at_x(k):
         return device(z, (x + k + 4) % 4, y, c)
 
-    sb, rb, accb, sbz, rbz = (sb0, sb1), (rb0, rb1), (accb0, accb1), (sbz0, sbz1), (rbz0, rbz1)
+    sb, rb, sc, rc = (sb0, sb1), (rb0, rb1), (sc0, sc1), (rc0, rc1)
+    accb, sbz, rbz = (accb0, accb1), (sbz0, sbz1), (rbz0, rbz1)
     across = device(z, x, 3 - y, c)
     beside = device(z, x, 2 * h + 1 - yl, c)
     mate = device(z, x, y, 1 - c)
@@ -128,7 +129,12 @@
     class AlongZX:
         def __init__(self, buf, rows, cols):
             self.buf, self.rows, self.cols = buf, rows, cols
-            self.spread = []
+            self.spread, self.relayed = [], []
+
+        def halves(self):
+            c0, w = self.cols
+            low = w // 256 * 128
+            return pl.ds(c0, low), pl.ds(c0 + low, w - low)
 
         def start(self):
             self.along_x(z)
@@ -136,15 +142,19 @@
 
         def along_x(self, zz):
             block = self.buf.at[zz, x, self.rows, pl.ds(*self.cols)]
-            self.spread += [send(block, block, at_x(k)) for k in (1, 3, 2)]
+            self.spread.append((zz, send(block, block, at_x(1)), send(block, block, at_x(-1))))
+
+        def relay(self, i):
+            zz, below, above = self.spread[i]
+            for copy, k, cols in zip((below, above), (1, -1), self.halves()):
+                copy.wait_recv()
+                block = self.buf.at[zz, (x - k + 4) % 4, self.rows, cols]
+                self.relayed.append(send(block, block, at_x(k)))
 
         def along_z(self, s):
-            c0, w = self.cols
-            a, b = ((c0, w), (c0, w)) if s < 4 else ((c0, w // 2), (c0 + w // 2, w // 2))
-            if s == 4 and w % 256:
-                a, b = (c0, w // 2 - 64), (c0 + w // 2 - 64, w // 2 + 64)
-            up = self.buf.at[(z - s + 9) % 8, x, self.rows, pl.ds(*a)]
-            down = self.buf.at[(z + s - 1) % 8, x, self.rows, pl.ds(*b)]
+            a, b = (pl.ds(*self.cols),) * 2 if s < 4 else self.halves()
+            up = self.buf.at[(z - s + 9) % 8, x, self.rows, a]
+            down = self.buf.at[(z + s - 1) % 8, x, self.rows, b]
             self.got = [send(up, up, at_z(1)), send(down, down, at_z(-1))]
 
         def next(self, s):
@@ -158,7 +168,7 @@
                 self.along_x((z + 4) % 8)
 
         def finish(self):
-            for copy in self.spread:
+            for copy in self.relayed:
                 copy.wait_recv()
 
     everything = pl.ds(0, 16)
@@ -250,21 +260,33 @@
             total += rax[j, k].astype(F32)
         g[:, pl.ds(*RS_A[j])] = total
 
-    first_x = [None] * 2
+    first_x, second_x = [None] * 2, [None] * 2
     last_z = [None] * 2
 
     def b_send(j):
+        cols = pl.ds(*RS_B[j])
         first_x[j] = []
-        for k in (1, 3, 2):
-            sb[j][k - 1] = gr[:, (x + k) % 4, :, pl.ds(*RS_B[j])].astype(BF16)
-            first_x[j].append(send(sb[j].at[k - 1], rb[j].at[k - 1], at_x(k)))
+        for way, k in ((0, 1), (1, -1)):
+            sb[j][way] = gr[pl.ds(4 * way, 4), (x + 2) % 4, :, cols].astype(BF16)
+            first_x[j].append(send(sb[j].at[way], rb[j].at[way], at_x(k)))
+
+    def b_pass(j):
+        cols = pl.ds(*RS_B[j])
+        second_x[j] = []
+        for way, k in ((0, 1), (1, -1)):
+            first_x[j][way].wait_recv()
+            to = (x + k + 4) % 4
+            part, rest = pl.ds(4 * way, 4), pl.ds(4 - 4 * way, 4)
+            sc[j][way, part] = (gr[part, to, :, cols] + rb[j][way].astype(F32)).astype(BF16)
+            sc[j][way, rest] = gr[rest, to, :, cols].astype(BF16)
+            second_x[j].append(send(sc[j].at[way], rc[j].at[way], at_x(k)))
 
     def b_turn(j):
-        for copy in first_x[j]:
+        for copy in second_x[j]:
             copy.wait_recv()
         total = gr[:, x, :, pl.ds(*RS_B[j])]
-        for k in range(3):
-            total += rb[j][k].astype(F32)
+        for way in range(2):
+            total += rc[j][way].astype(F32)
         accb[j][...] = total
         last_z[j] = []
         for k in (4, 3, 5, 2, 6, 1, 7):
@@ -372,99 +394,125 @@
         ugv[:, cols] = (dhid * (gate * sig)).astype(BF16)
         ggv[:, cols] = (dhid * uv[:, cols].astype(F32) * sig * (1.0 + gate * (1.0 - sig))).astype(BF16)
 
-    w_a[1].start()
     take(0)
+    take(1)
     w_b.start()
     w_a[0].start()
+    take(2)
+    w_a[1].start()
+    pass_on(0)
     hide()
-    w_a[0].next(0)
+    take(3)
+    w_b.next(1)
+    pass_on(1)
+    w_b.next(2)
+    w_b.relay(0)
+    w_b.relay(3)
+    pass_on(3)
     w_a[1].next(0)
-    take(1)
-    pass_on(0)
-    w_b.next(1)
-    take(2)
-    w_a[0].next(1)
-    take(3)
-    w_a[1].next(1)
-    pass_on(1)
     pass_on_again(0)
-    w_b.next(2)
+    pass_on_again(1)
+    w_b.next(3)
+    pass_on(2)
     partial_sums(0)
-    pass_on(3)
-    w_a[0].next(2)
     b_send(0)
-    pass_on_again(1)
+    partial_sums(1)
     pass_on_again(3)
-    partial_sums(1)
     a_send(0, 1)
-    w_b.next(3)
     partial_sums(3)
     a_send(1, 1)
+    pass_on_again(2)
+    w_a[0].next(0)
     a_send(0, 2)
-    pass_on(2)
+    partial_sums(2)
     a_send(1, 2)
-    pass_on_again(2)
+    w_a[0].next(1)
     a_send(0, 3)
+    b_send(1)
     a_send(1, 3)
-    partial_sums(2)
+    b_pass(0)
+    a_send(0, 4)
+    b_pass(1)
+    w_b.relay(4)
+    a_send(1, 4)
+    w_b.next(4)
+    w_a[1].next(1)
     b_turn(0)
-    a_send(0, 4)
-    b_send(1)
-    w_b.next(4)
-    a_send(1, 4)
     b_turn(1)
-    b_end(0)
     w_a[1].next(2)
-    w_a[0].next(3)
     a_turn(0)
     a_turn(1)
+    b_end(0)
+    w_a[1].next(3)
+    a_end(1)
+    w_a[0].next(2)
+    w_b.relay(2)
+    b_end(1)
+    w_b.relay(1)
     a_end(0)
-    b_end(1)
-    a_end(1)
     squares()
+    w_b.relay(5)
+    w_a[0].next(3)
     squares_x()
-    w_a[1].next(3)
     squares_y()
+    w_b.relay(7)
+    w_a[1].next(4)
     adam()
-    w_a[1].next(4)
+    n_c[1].start()
+    w_b.relay(6)
+    n_b[0].start()
     swap_rows()
+    n_c[0].start()
+    n_c[1].next(0)
     w_a[0].next(4)
-    n_c[1].start()
-    n_b[0].start()
-    n_c[0].start()
+    n_b[0].next(1)
+    swapped_rows()
     d_hidden(1)
-    n_b[0].next(1)
-    n_c[1].next(0)
-    n_c[0].next(0)
-    swapped_rows()
     n_b[1].start()
-    d_hidden(0)
+    n_b[0].relay(0)
     n_c[1].next(1)
     n_b[0].next(2)
+    n_c[0].next(0)
     n_b[1].next(1)
+    n_a.next(0)
     n_c[0].next(1)
-    n_a.next(0)
+    n_b[0].next(3)
+    d_hidden(0)
     n_c[1].next(2)
+    turn_back()
     n_b[1].next(2)
+    n_b[0].relay(3)
+    n_a.next(1)
+    n_b[0].relay(1)
+    n_b[1].relay(1)
+    n_b[0].relay(4)
+    n_b[0].relay(5)
+    n_b[0].next(4)
     n_c[0].next(2)
-    n_b[0].next(3)
-    n_a.next(1)
+    n_b[1].next(3)
+    n_b[1].relay(2)
+    n_b[1].relay(3)
+    n_b[1].relay(0)
     n_c[1].next(3)
-    turn_back()
-    n_b[1].next(3)
     n_a.next(2)
+    n_b[0].relay(2)
+    n_c[0].next(3)
+    n_c[1].next(4)
     gradients(0)
-    n_c[1].next(4)
+    n_b[1].next(4)
     gradients(1)
-    n_c[0].next(3)
-    n_b[1].next(4)
     gradients(2)
-    n_b[0].next(4)
+    n_b[1].relay(6)
     n_a.next(3)
+    n_b[0].relay(6)
+    n_b[1].relay(5)
     gradients(3)
+    n_b[0].relay(7)
     gradients(4)
     n_c[0].next(4)
+    n_b[1].relay(7)
     gradients(5)
+    n_b[1].relay(4)
     gradients(6)
     n_a.next(4)
     gradients(7)
@@ -521,7 +569,7 @@
                 vm(leaf, kind)
                 for _, wb in RS_B
                 for leaf, kind in (
-                    ((3, 8, 16, wb), BF16), ((3, 8, 16, wb), BF16), ((8, 16, wb), F32),
+                    ((2, 4, 16, wb), BF16), ((2, 4, 16, wb), BF16), ((2, 8, 16, wb), BF16), ((2, 8, 16, wb), BF16), ((8, 16, wb), F32),
                     ((7, 16, wb), BF16), ((7, 16, wb), BF16),
                 )
             ),

time: 119 us -> 114 us (0.958)
  Pallas kernels: 118 us -> 114 us
    pallas_call x1, Pallas kernels: 114 us -> 110 us  [on_device(): pl.pallas_call(kernel, out_shape=tuple((vm(*leaf) for leaf in shapes)), i...]
where the time goes in v5:
time: 114 us
  Pallas kernels  114 us (100%)
    pallas_call x1, Pallas kernels, on_device(): pl.pallas_call(kernel, out_shape=tuple((vm(*leaf) for leaf in shapes)), i...  110 us
    pallas_call x1, Pallas kernels, on_device(): pl.pallas_call(store, out_shape=tuple((shape(*leaf) for leaf in shapes)),...  3.25 us

profile of v5, /device:TPU:8, one launch (start us, length us, event | category | flops | bytes accessed | tf_op | source)
XLA Modules:
  0.0 114.4 jit_solution(9148315460785242006)
XLA Ops:
  0.6 110.5 %step.1 = (bf16[256,1024]{1,0:T(8,128)(2,1)S(1)}, bf16[256,1024]{1,0:T(8,128)(2,1)S(1)}, f32[16,3072]{1,0:T(8,128)S(1)}, f32[16,3072]{1,0:T(8,128)S(1)}, f32[16,...) custom-call(bf16[256,3072]{1,0:T(8,128)(2,1)} %d_in.1, bf16[256,1024]{1,0:T(8,128)(2,1)} %g_in.1, ...), custom_call_target="tpu_custom_call" | custom-call | tf_op jit(solution)/shard_map/step/pallas_call | solution.py:545
  111.1 3.3 %store.1 = (bf16[256,1024]{1,0:T(8,128)(2,1)}, bf16[256,1024]{1,0:T(8,128)(2,1)}, f32[16,3072]{1,0:T(8,128)}, f32[16,3072]{1,0:T(8,128)}, f32[16,3072]{1,0:T(8,128)}, /*index=5*/bf16[8,4,32,3072]{3,2,1,0:T(8,128)(2,1)}) custom-call(bf16[256,1024]{1,0:T(8,128)(2,1)S(1)} %get-tuple-element.18.refs_0_, bf16[256,1024]{1,0:T(8,128)(2,1)S(1)} %get-tuple-element.19.refs_1_, ...), custom_call_target="tpu_custom_call" | custom-call | tf_op jit(solution)/shard_map/store/pallas_call | solution.py:594

commit v6 on v5

--- a/solution.py
+++ b/solution.py
@@ -16,9 +16,9 @@
 RS_A = ((768, 768), (2304, 768))
 RS_B = ((0, 768), (1536, 768))
 CHUNKS = (RS_B[0], RS_A[0], RS_B[1], RS_A[1])
-W_A = ((0, 128), (128, 128))
-W_B = (256, 2816)
-N_C = ((0, 384), (384, 640))
+W_A = ((0, 128), (128, 384))
+W_B = (512, 2560)
+N_C = ((0, 256), (256, 768))
 N_A = (1024, 384)
 N_B = (1408, 1664)
 N_SWAP = (1024, 2048)
@@ -396,126 +396,126 @@
 
     take(0)
     take(1)
+    take(2)
+    w_a[0].start()
+    w_a[1].start()
     w_b.start()
-    w_a[0].start()
-    take(2)
-    w_a[1].start()
     pass_on(0)
+    w_a[0].next(0)
+    take(3)
     hide()
-    take(3)
     w_b.next(1)
     pass_on(1)
+    w_a[0].next(1)
+    w_a[1].next(0)
     w_b.next(2)
-    w_b.relay(0)
-    w_b.relay(3)
+    w_a[1].next(1)
+    pass_on_again(1)
     pass_on(3)
-    w_a[1].next(0)
+    w_a[0].next(2)
+    w_b.next(3)
     pass_on_again(0)
-    pass_on_again(1)
-    w_b.next(3)
-    pass_on(2)
     partial_sums(0)
-    b_send(0)
     partial_sums(1)
     pass_on_again(3)
+    b_send(0)
     a_send(0, 1)
+    pass_on(2)
     partial_sums(3)
     a_send(1, 1)
+    a_send(0, 2)
     pass_on_again(2)
-    w_a[0].next(0)
-    a_send(0, 2)
+    w_b.relay(3)
+    b_pass(0)
+    a_send(1, 2)
     partial_sums(2)
-    a_send(1, 2)
-    w_a[0].next(1)
+    w_a[0].next(3)
     a_send(0, 3)
     b_send(1)
     a_send(1, 3)
-    b_pass(0)
+    b_turn(0)
+    w_a[0].next(4)
     a_send(0, 4)
     b_pass(1)
+    w_b.relay(1)
+    a_send(1, 4)
     w_b.relay(4)
-    a_send(1, 4)
-    w_b.next(4)
-    w_a[1].next(1)
-    b_turn(0)
     b_turn(1)
+    w_b.relay(5)
+    a_turn(1)
+    w_b.relay(6)
+    a_turn(0)
     w_a[1].next(2)
-    a_turn(0)
-    a_turn(1)
+    w_b.relay(2)
     b_end(0)
     w_a[1].next(3)
     a_end(1)
-    w_a[0].next(2)
-    w_b.relay(2)
+    w_b.next(4)
     b_end(1)
-    w_b.relay(1)
     a_end(0)
     squares()
-    w_b.relay(5)
-    w_a[0].next(3)
+    w_b.relay(0)
+    w_a[1].next(4)
     squares_x()
     squares_y()
     w_b.relay(7)
-    w_a[1].next(4)
     adam()
+    n_c[0].start()
+    swap_rows()
+    n_b[0].start()
     n_c[1].start()
-    w_b.relay(6)
-    n_b[0].start()
-    swap_rows()
-    n_c[0].start()
+    d_hidden(1)
+    n_b[0].next(1)
+    n_c[0].next(0)
+    swapped_rows()
     n_c[1].next(0)
-    w_a[0].next(4)
-    n_b[0].next(1)
-    swapped_rows()
-    d_hidden(1)
     n_b[1].start()
+    n_b[0].next(2)
+    n_c[0].next(1)
+    d_hidden(0)
     n_b[0].relay(0)
     n_c[1].next(1)
-    n_b[0].next(2)
-    n_c[0].next(0)
+    n_b[0].relay(1)
     n_b[1].next(1)
+    turn_back()
+    n_b[0].next(3)
     n_a.next(0)
-    n_c[0].next(1)
-    n_b[0].next(3)
-    d_hidden(0)
-    n_c[1].next(2)
-    turn_back()
+    n_c[0].next(2)
     n_b[1].next(2)
     n_b[0].relay(3)
+    n_c[1].next(2)
+    n_b[1].relay(2)
+    n_b[0].next(4)
+    n_b[0].relay(4)
+    n_b[1].relay(1)
+    n_c[0].next(3)
     n_a.next(1)
-    n_b[0].relay(1)
-    n_b[1].relay(1)
-    n_b[0].relay(4)
-    n_b[0].relay(5)
-    n_b[0].next(4)
-    n_c[0].next(2)
     n_b[1].next(3)
-    n_b[1].relay(2)
-    n_b[1].relay(3)
+    n_c[1].next(3)
+    n_b[1].relay(4)
     n_b[1].relay(0)
-    n_c[1].next(3)
     n_a.next(2)
-    n_b[0].relay(2)
-    n_c[0].next(3)
-    n_c[1].next(4)
+    n_b[1].next(4)
+    n_b[1].relay(6)
+    n_b[0].relay(6)
     gradients(0)
-    n_b[1].next(4)
+    n_b[1].relay(5)
+    n_b[0].relay(7)
     gradients(1)
     gradients(2)
-    n_b[1].relay(6)
-    n_a.next(3)
-    n_b[0].relay(6)
-    n_b[1].relay(5)
-    gradients(3)
-    n_b[0].relay(7)
-    gradients(4)
     n_c[0].next(4)
     n_b[1].relay(7)
+    gradients(3)
+    n_c[1].next(4)
+    gradients(4)
+    n_a.next(3)
+    n_b[0].relay(5)
     gradients(5)
-    n_b[1].relay(4)
     gradients(6)
+    n_b[0].relay(2)
+    n_b[1].relay(3)
+    gradients(7)
     n_a.next(4)
-    gradients(7)
     for part in (*n_b, *n_c):
         part.finish()
     for copy in sent:

time: 114 us -> 115 us (level)
  no operation moved by 1% of the time
where the time goes in v6:
time: 115 us
  Pallas kernels  115 us (100%)
    pallas_call x1, Pallas kernels, on_device(): pl.pallas_call(kernel, out_shape=tuple((vm(*leaf) for leaf in shapes)), i...  111 us
    pallas_call x1, Pallas kernels, on_device(): pl.pallas_call(store, out_shape=tuple((shape(*leaf) for leaf in shapes)),...  3.25 us

profile of v6, /device:TPU:8, one launch (start us, length us, event | category | flops | bytes accessed | tf_op | source)
XLA Modules:
  0.0 115.3 jit_solution(14622634089083370727)
XLA Ops:
  0.6 111.4 %step.1 = (bf16[256,1024]{1,0:T(8,128)(2,1)S(1)}, bf16[256,1024]{1,0:T(8,128)(2,1)S(1)}, f32[16,3072]{1,0:T(8,128)S(1)}, f32[16,3072]{1,0:T(8,128)S(1)}, f32[16,...) custom-call(bf16[256,3072]{1,0:T(8,128)(2,1)} %d_in.1, bf16[256,1024]{1,0:T(8,128)(2,1)} %g_in.1, ...), custom_call_target="tpu_custom_call" | custom-call | tf_op jit(solution)/shard_map/step/pallas_call | solution.py:545
  112.0 3.3 %store.1 = (bf16[256,1024]{1,0:T(8,128)(2,1)}, bf16[256,1024]{1,0:T(8,128)(2,1)}, f32[16,3072]{1,0:T(8,128)}, f32[16,3072]{1,0:T(8,128)}, f32[16,3072]{1,0:T(8,128)}, /*index=5*/bf16[8,4,32,3072]{3,2,1,0:T(8,128)(2,1)}) custom-call(bf16[256,1024]{1,0:T(8,128)(2,1)S(1)} %get-tuple-element.18.refs_0_, bf16[256,1024]{1,0:T(8,128)(2,1)S(1)} %get-tuple-element.19.refs_1_, ...), custom_call_target="tpu_custom_call" | custom-call | tf_op jit(solution)/shard_map/store/pallas_call | solution.py:594
